TPU v7x, 256 devices: a whole 4x4x8 slice. The times are simulated.
256 devices in a mesh: req: 4 (over x_hi, core), tp: 64 (over z, x_lo, y).
Axes of the slice: x: 4 (x_hi: 2, x_lo: 2; x = x_hi * 2 + x_lo), y: 4, z: 8, core: 2. Of those that a mesh axis runs over, the one named last changes fastest.
Arguments:
- hidden: bfloat16 [4096, 8192], P('req', 'tp'), may hold values from -6 to 6
- query_weight: bfloat16 [8192, 8192], P(None, 'tp'), may hold values from -0.0625 to 0.0625
- key_value_weight: bfloat16 [8192, 2048], P(None, 'tp'), may hold values from -0.0625 to 0.0625
- adapter_down_maps: bfloat16 [64, 8192, 32], P('req', 'tp'), may hold values from -0.0625 to 0.0625
- adapter_up_maps: bfloat16 [64, 32, 8192], P('req', None, 'tp'), may hold values from -1 to 1
- token_request_start: int32 [4096], P('req'), may hold values from 0 to 31, as said below
- adapter_per_block: int32 [32], P('req'), may hold values from 0 to 63
Outputs:
- context: bfloat16 [4096, 8192], P('req', 'tp')
Inputs may be any that keep to these rules, and one draw needn't show every extreme that they name: `token_request_start`: each run of 1024 tokens along the req split holds whole requests; a request is a run of whole blocks of 128 tokens; the last block of each such run is a request of its own.
All inputs are finite; a program needn't handle non-finite values.
Results may differ from a plain program's by a relative error of at most 0.012.
Values may be sent and summed in bfloat16 or wider, within the bound.
No kernel may reach another device: no remote copies, remote signals or barrier semaphores. Data moves between devices by JAX's collectives and lax.ppermute only.
A program may use at most 64 MiB of HBM per device.

v0:
```python
import math
import jax
import jax.numpy as jnp
from jax import lax
from jax.sharding import PartitionSpec as P

HEAD_SIZE = 128
BLOCK = 128
ROPE_BASE = 500000.0
ADAPTER_SCALE = 2.0


def from_partner(block, axis, bit):
    count = lax.axis_size(axis)
    route = []
    for low in range(count):
        high = low | 1 << bit
        if high != low and high < count:
            route += [(low, high), (high, low)]
    return lax.ppermute(block, axis, route)


def rotate(vectors, positions):
    half_width = vectors.shape[-1] // 2
    steps_half = jnp.arange(half_width, dtype=jnp.float32)
    inverse = jnp.exp(-(2.0 * steps_half / vectors.shape[-1]) * math.log(ROPE_BASE))
    angles = positions.astype(jnp.float32)[:, None] * inverse[None, :]
    cosines = jnp.cos(angles)
    sines = jnp.sin(angles)
    front_half = vectors[:, :half_width]
    back_half = vectors[:, half_width:]
    return jnp.concatenate(
        [front_half * cosines - back_half * sines, back_half * cosines + front_half * sines], axis=1
    )


def attend(queries, key_rows, value_rows, request):
    group_rows = queries.shape[0]
    block_rows = min(512, group_rows)
    block_total = group_rows // block_rows
    places = jnp.arange(group_rows, dtype=jnp.int32)
    score_scale = 1.0 / math.sqrt(queries.shape[1])

    def one_block(block_index):
        begin_row = block_index * block_rows
        q_blk = lax.dynamic_slice_in_dim(queries, begin_row, block_rows, 0)
        r_blk = lax.dynamic_slice_in_dim(request, begin_row, block_rows, 0)
        p_blk = lax.dynamic_slice_in_dim(places, begin_row, block_rows, 0)
        scores = (
            lax.dot_general(
                q_blk, key_rows, (((1,), (1,)), ((), ())), preferred_element_type=jnp.float32
            )
            * score_scale
        )
        allowed = (r_blk[:, None] == request[None, :]) & (places[None, :] <= p_blk[:, None])
        scores = jnp.where(allowed, scores, jnp.float32(-1e30))
        row_max = jnp.max(scores, axis=1, keepdims=True)
        weights = jnp.exp(scores - row_max)
        probs = (weights / jnp.sum(weights, axis=1, keepdims=True)).astype(jnp.bfloat16)
        return jnp.dot(probs, value_rows, preferred_element_type=jnp.float32).astype(jnp.bfloat16)

    blocks = lax.map(one_block, jnp.arange(block_total, dtype=jnp.int32))
    return blocks.reshape(group_rows, value_rows.shape[1])


def body(
    hidden,
    query_weight,
    key_value_weight,
    adapter_down_maps,
    adapter_up_maps,
    token_request_start,
    adapter_per_block,
):
    group_rows = hidden.shape[0]
    local_width = hidden.shape[1]
    head_cols = query_weight.shape[1]
    kv_cols = key_value_weight.shape[1]
    device = lax.axis_index("tp")
    spread = 2 * HEAD_SIZE // kv_cols
    piece = lax.all_gather(hidden, "tp", axis=1, tiled=True)
    query_total = jnp.dot(piece, query_weight, preferred_element_type=jnp.float32)
    kv_sum = jnp.dot(piece, key_value_weight, preferred_element_type=jnp.float32)
    down_all, up_all = (
        lax.all_gather(adapter_down_maps, "req", axis=0, tiled=True),
        lax.all_gather(adapter_up_maps, "req", axis=0, tiled=True),
    )
    block_total = group_rows // BLOCK
    chosen_down = down_all[adapter_per_block]
    chosen_up = up_all[adapter_per_block]
    block_grouped = hidden.reshape(block_total, BLOCK, local_width)
    reduced_part = jnp.einsum(
        "uqo,uop->uqp", block_grouped, chosen_down, preferred_element_type=jnp.float32
    )
    reduced_rank = lax.psum(reduced_part, "tp").astype(jnp.bfloat16)
    adapter_term = jnp.einsum(
        "epl,elm->epm", reduced_rank, chosen_up, preferred_element_type=jnp.float32
    ).reshape(group_rows, head_cols)
    places = lax.axis_index("req") * group_rows + jnp.arange(group_rows, dtype=jnp.int32)
    positions = places - token_request_start * BLOCK
    complete_query = query_total + ADAPTER_SCALE * adapter_term
    kv_piece = kv_sum.astype(jnp.bfloat16)
    head_block = kv_piece
    for bit_number in range(spread.bit_length() - 1):
        partner = from_partner(head_block, "tp", bit_number)
        upper_side = device // 2**bit_number % 2
        head_block = jnp.where(
            upper_side == 1,
            jnp.concatenate([partner, head_block], axis=1),
            jnp.concatenate([head_block, partner], axis=1),
        )
    key_rows = rotate(head_block[:, :HEAD_SIZE].astype(jnp.float32), positions).astype(jnp.bfloat16)
    value_rows = head_block[:, HEAD_SIZE:]
    head_query = rotate(complete_query, positions).astype(jnp.bfloat16)
    outputs = attend(head_query, key_rows, value_rows, token_request_start)
    return outputs


def solution(mesh):
    in_specs = (
        P("req", "tp"),
        P(None, "tp"),
        P(None, "tp"),
        P("req", "tp", None),
        P("req", None, "tp"),
        P("req"),
        P("req"),
    )
    out_specs = P("req", "tp")
    return jax.shard_map(body, mesh=mesh, in_specs=in_specs, out_specs=out_specs, check_vma=False)
```

profile of v0, /device:TPU:4, one launch (start us, length us, event | category | flops | bytes accessed | tf_op | source)
XLA Modules:
  0.0 415.5 jit_solution(10693275927732517615)
XLA Ops:
  6.5 0.7 all-gather.2.cloned.1.call-update
  7.3 0.7 compare_select_fusion
  8.0 8.5 %all_gather.10 = bf16[64,128,32]{1,2,0:T(8,128)(2,1)S(1)} all-gather(bf16[16,128,32]{1,2,0:T(8,128)(2,1)} %param.12), channel_id=1, replica_groups=mesh['req'=4,'tp'=64] {'req'}, dimensions={0}, use_global_device_ids=true | all-gather | bytes 655360 | tf_op jit(solution)/shard_map/all_gather | solution.py:85
  16.5 0.6 gather_fusion
  17.0 1.2 convolution_bitcast_fusion
  18.2 11.8 %all_gather.11 = bf16[64,32,128]{2,1,0:T(8,128)(2,1)S(1)} all-gather(bf16[16,32,128]{2,1,0:T(8,128)(2,1)} %param.13), channel_id=1, replica_groups=mesh['req'=4,'tp'=64] {'req'}, dimensions={0}, use_global_device_ids=true | all-gather | bytes 655360 | tf_op jit(solution)/shard_map/all_gather | solution.py:86
  30.0 0.6 gather_fusion.1
  30.6 314.2 %all-reduce.1 = bf16[8,128,32]{1,2,0:T(8,128)(2,1)S(1)} all-reduce(f32[8,128,32]{1,2,0:T(8,128)S(1)} %convolution_bitcast_fusion), channel_id=1, replica_groups=mesh['req'=4,'tp'=64] {'tp'}, use_global_device_ids=true, to_apply=%region_0.0 | all-reduce | flops 32768 | bytes 196608 | tf_op jit(solution)/shard_map/psum | solution.py:95
  344.8 13.7 %all-gather.2.cloned.1.call-done = bf16[1024,8192]{1,0:T(8,128)(2,1)} async-done(((bf16[1024,128]{1,0:T(8,128)(2,1)}), bf16[1024,8192]{1,0:T(8,128)(2,1)}) %all-gather.2.cloned.1.call-update) | async-done | bytes 16777232 | tf_op jit(solution)/shard_map/all_gather | solution.py:81
  358.5 10.8 %convolution_convert_fusion.1 = bf16[1024,32]{0,1:T(8,128)(2,1)S(1)} fusion(bf16[1024,8192]{1,0:T(8,128)(2,1)} %all-gather.2.cloned.1.call-done, bf16[8192,32]{0,1:T(8,128)(2,1)S(1)} %copy-done.1), kind=kOutput, calls=%fused_computation.14 | convolution fusion | flops 536903680 | bytes 17367040 | tf_op jit(solution)/shard_map/dot_general | solution.py:83
  369.3 0.5 collective-permute-start
  369.9 0.3 convolution_multiply_fusion
  370.2 3.5 collective-permute-done
  373.7 6.2 %collective-permute-start.1 = (bf16[1024,64]{0,1:T(8,128)(2,1)S(1)}, bf16[1024,64]{0,1:T(8,128)(2,1)}, u32[]{:S(2)}, u32[]{:S(2)}) collective-permute-start(bf16[1024,64]{0,1:T(8,128)(2,1)S(1)} %maximum_select_fusion.2), channel_id=1, source_target_pairs={{0,2},{2,0},{1,3},{3,1},{4,6},{6,4},{5,7},{7,5},{8,10},{10,8},{9,1... | collective-permute-start | bytes 393224 | tf_op jit(solution)/shard_map/ppermute | solution.py:20
  379.8 0.2 copy.16
  380.0 2.8 collective-permute-done.1
  382.9 1.0 maximum_select_fusion.1
  383.9 3.0 collective-permute-start.2
  386.9 11.4 %convolution_add_fusion = f32[1024,128]{0,1:T(8,128)S(1)} fusion(f32[1024,128]{0,1:T(8,128)S(1)} %copy.16, bf16[1024,8192]{1,0:T(8,128)(2,1)} %all-gather.2.cloned.1.call-done, bf16[8192,128]{1,0:T(8,128)(2,1)S(1)} %copy-done), kind=kOutput, calls=%fused_computation.12 | convolution fusion | flops 2147614720 | bytes 19922944 | tf_op jit(solution)/shard_map/dot_general | solution.py:82
  398.3 1.2 maximum_select_fusion
  399.6 1.2 fusion.18
  401.1 0.2 copy.15
  401.3 6.7 %while.11 = (s32[]{:T(128)}, bf16[2,512,128]{2,1,0:T(8,128)(2,1)S(1)}, s32[2]{0:T(128)S(1)}, s32[1024]{0:T(1024)S(1)}, s32[1024]{0:T(1024)S(1)}, /*index=5*/bf16...) while((s32[]{:T(128)}, ...), condition=%wide.region_4.5_spmd.clone, body=%wide.region_1.4_spmd.clone.sunk | while | flops 274267136 | bytes 7108799 | solution.py:62
  401.3 0.6 dynamic_slice.26
  402.7 0.8 fusion.41
  403.5 0.5 fusion.42
  404.0 0.6 fusion.43
  404.6 0.6 dynamic_slice.26
  406.0 0.8 fusion.41
  406.8 0.5 fusion.42
  407.3 0.6 fusion.43
  408.0 0.7 copy-done.4
  (25 shorter events, 0.7 us)
Async XLA Ops:
  6.5 380.4 %copy-start = (bf16[8192,128]{1,0:T(8,128)(2,1)S(1)}, bf16[8192,128]{1,0:T(8,128)(2,1)}, u32[]{:S(2)}) copy-start(bf16[8192,128]{1,0:T(8,128)(2,1)} %param.10) | copy-start | bytes 6291460
  6.5 352.0 %copy-start.1 = (bf16[8192,32]{0,1:T(8,128)(2,1)S(1)}, bf16[8192,32]{0,1:T(8,128)(2,1)}, u32[]{:S(2)}) copy-start(bf16[8192,32]{0,1:T(8,128)(2,1)} %param.11) | copy-start | bytes 1572868
  6.5 352.0 %all-gather.2.cloned.1.call-start = ((), (), s32[]{:S(2)}) async-start(), calls=%async_computation | async-start | bytes 17039360 | tf_op jit(solution)/shard_map/all_gather | solution.py:81
  344.8 35.0 %copy-start.2 = (s32[1024]{0:T(1024)S(1)}, s32[1024]{0:T(1024)}, u32[]{:S(2)}) copy-start(s32[1024]{0:T(1024)} %param.14) | copy-start | bytes 12292
  369.3 4.3 %collective-permute-start = (bf16[1024,32]{0,1:T(8,128)(2,1)S(1)}, bf16[1024,32]{0,1:T(8,128)(2,1)S(1)}, u32[]{:S(2)}, u32[]{:S(2)}) collective-permute-start(bf16[1024,32]{0,1:T(8,128)(2,1)S(1)} %convolution_convert_fusion.1), channel_id=1, source_target_pairs={{0,1},{1,0},{2,3},{3,2},{4,5},{5,4},{6,7},{7,6},{8,9},{9,8},{10,11... | collective-permute-start | bytes 196616 | tf_op jit(solution)/shard_map/ppermute | solution.py:20
  373.7 9.2 %collective-permute-start.1 = (bf16[1024,64]{0,1:T(8,128)(2,1)S(1)}, bf16[1024,64]{0,1:T(8,128)(2,1)}, u32[]{:S(2)}, u32[]{:S(2)}) collective-permute-start(bf16[1024,64]{0,1:T(8,128)(2,1)S(1)} %maximum_select_fusion.2), channel_id=1, source_target_pairs={{0,2},{2,0},{1,3},{3,1},{4,6},{6,4},{5,7},{7,5},{8,10},{10,8},{9,1... | collective-permute-start | bytes 393224 | tf_op jit(solution)/shard_map/ppermute | solution.py:20
  383.9 14.4 %collective-permute-start.2 = (bf16[1024,128]{0,1:T(8,128)(2,1)S(1)}, bf16[1024,128]{0,1:T(8,128)(2,1)}, u32[]{:S(2)}, u32[]{:S(2)}) collective-permute-start(bf16[1024,128]{0,1:T(8,128)(2,1)S(1)} %maximum_select_fusion.1), channel_id=1, source_target_pairs={{0,4},{4,0},{1,5},{5,1},{2,6},{6,2},{3,7},{7,3},{8,12},{12,8},{9,1... | collective-permute-start | bytes 786440 | tf_op jit(solution)/shard_map/ppermute | solution.py:20
  399.6 1.7 copy-start.3
  408.0 0.7 copy-start.4
Sparse Core Ops, SparseCore 0:
  9.1 349.3 all-gather.1
where the time goes:
time: 416 us
  blocking collectives  335 us (81%)
  matrix products  26.5 us (6%)
  waiting for transfers between devices  20.7 us (5%)
  between operations  13.6 us (3%)
  starting transfers between devices  9.68 us (2%)
  other arithmetic  5.36 us (1%)
    psum x1, blocking collectives, body(): reduced_rank = lax.psum(reduced_part, 'tp').astype(jnp.bfloat16)  314 us
    all_gather x1, waiting for transfers between devices, body(): piece = lax.all_gather(hidden, 'tp', axis=1, tiled=True)  13.7 us
    all_gather x1, blocking collectives, body(): lax.all_gather(adapter_up_maps, 'req', axis=0, tiled=True)  11.8 us
    dot_general x1, matrix products, body(): jnp.dot(piece, query_weight, preferred_element_type=jnp.float32)  11.4 us
    dot_general x1, matrix products, body(): jnp.dot(piece, key_value_weight, preferred_element_type=jnp.float32)  10.8 us
    ppermute x3, starting transfers between devices, from_partner(): return lax.ppermute(block, axis, route)  9.68 us
    all_gather x1, blocking collectives, body(): lax.all_gather(adapter_down_maps, 'req', axis=0, tiled=True)  8.48 us
  transfers between devices with their start and end apart: 4, of which 3 were waited for; matrix products, arithmetic and copies ran while one was open for 4% of the time, Pallas kernels for 0%

commit v1 on v0

--- a/solution.py
+++ b/solution.py
@@ -8,6 +8,13 @@
 BLOCK = 128
 ROPE_BASE = 500000.0
 ADAPTER_SCALE = 2.0
+
+
+def all_by_exchange(x, mesh_axis, dim):
+    size = lax.axis_size(mesh_axis)
+    blocks = jnp.stack([x for _ in range(size)])
+    blocks = lax.all_to_all(blocks, mesh_axis, split_axis=0, concat_axis=0)
+    return jnp.concatenate(blocks, axis=dim)
 
 
 def from_partner(block, axis, bit):
@@ -82,7 +89,7 @@
     query_total = jnp.dot(piece, query_weight, preferred_element_type=jnp.float32)
     kv_sum = jnp.dot(piece, key_value_weight, preferred_element_type=jnp.float32)
     down_all, up_all = (
-        lax.all_gather(adapter_down_maps, "req", axis=0, tiled=True),
+        all_by_exchange(adapter_down_maps, "req", 0),
         lax.all_gather(adapter_up_maps, "req", axis=0, tiled=True),
     )
     block_total = group_rows // BLOCK

time: 416 us -> 715 us (1.72)
  waiting for transfers between devices: 20.7 us -> 337 us
  blocking collectives: 335 us -> 318 us
    all_gather x1, waiting for transfers between devices: 13.7 us -> 331 us  [body(): piece = lax.all_gather(hidden, 'tp', axis=1, tiled=True)]
    all_gather x1 -> x0, blocking collectives: 8.48 us -> none  [body(): lax.all_gather(adapter_down_maps, 'req', axis=0, tiled=True)]
    ppermute x3, starting transfers between devices: 9.68 us -> 2.08 us  [from_partner(): return lax.ppermute(block, axis, route)]
    psum x1, blocking collectives: 314 us -> 307 us  [body(): reduced_rank = lax.psum(reduced_part, 'tp').astype(jnp.bfloat16)]
  transfers between devices with their start and end apart: 4 -> 5, of which waited for: 3 -> 2; matrix products, arithmetic and copies ran while one was open for 4% -> 2% of each run, Pallas kernels for 0% -> 0%
where the time goes in v1:
time: 715 us; the launch traced here: 714 us
  waiting for transfers between devices  337 us (47%)
  blocking collectives  318 us (44%)
  matrix products  25.6 us (4%)
  between operations  13.6 us (2%)
  starting transfers between devices  7.8 us (1%)
    all_gather x1, waiting for transfers between devices, body(): piece = lax.all_gather(hidden, 'tp', axis=1, tiled=True)  331 us
    psum x1, blocking collectives, body(): reduced_rank = lax.psum(reduced_part, 'tp').astype(jnp.bfloat16)  307 us
  transfers between devices with their start and end apart: 5, of which 2 were waited for; matrix products, arithmetic and copies ran while one was open for 2% of the time, Pallas kernels for 0%

profile of v1, /device:TPU:4, one launch (start us, length us, event | category | flops | bytes accessed | tf_op | source)
XLA Modules:
  0.0 714.4 jit_solution(6484012440040664613)
XLA Ops:
  6.6 0.7 all-gather.2.cloned.1.call-update
  7.3 1.9 stack.2
  9.1 5.7 all-to-all-start
  14.8 10.8 %all_gather.7 = bf16[64,32,128]{2,1,0:T(8,128)(2,1)S(1)} all-gather(bf16[16,32,128]{2,1,0:T(8,128)(2,1)S(1)} %copy-done.3), channel_id=1, replica_groups=mesh['req'=4,'tp'=64] {'req'}, dimensions={0}, use_global_device_ids=true | all-gather | bytes 655360 | tf_op jit(solution)/shard_map/all_gather | solution.py:93
  25.7 1.2 gather_fusion.1
  26.9 0.6 gather_fusion
  27.5 0.2 convolution_bitcast_fusion
  27.7 330.6 %all-gather.2.cloned.1.call-done = bf16[1024,8192]{1,0:T(8,128)(2,1)} async-done(((bf16[1024,128]{1,0:T(8,128)(2,1)}), bf16[1024,8192]{1,0:T(8,128)(2,1)}) %all-gather.2.cloned.1.call-update) | async-done | bytes 16777232 | tf_op jit(solution)/shard_map/all_gather | solution.py:88
  358.4 10.9 %convolution_convert_fusion.1 = bf16[1024,32]{0,1:T(8,128)(2,1)S(1)} fusion(bf16[1024,8192]{1,0:T(8,128)(2,1)} %all-gather.2.cloned.1.call-done, bf16[8192,32]{0,1:T(8,128)(2,1)} %param.11), kind=kOutput, calls=%fused_computation.14 | convolution fusion | flops 536903680 | bytes 17367040 | tf_op jit(solution)/shard_map/dot_general | solution.py:90
  369.2 1.7 collective-permute-start
  370.9 306.8 %all-reduce.1 = bf16[8,128,32]{1,2,0:T(8,128)(2,1)S(1)} all-reduce(f32[8,128,32]{1,2,0:T(8,128)S(1)} %convolution_bitcast_fusion), channel_id=1, replica_groups=mesh['req'=4,'tp'=64] {'tp'}, use_global_device_ids=true, to_apply=%region_0.0 | all-reduce | flops 32768 | bytes 196608 | tf_op jit(solution)/shard_map/psum | solution.py:102
  677.8 0.1 collective-permute-start.1
  677.9 0.3 convolution_multiply_fusion
  678.2 0.2 copy.17
  678.4 6.1 collective-permute-done.1
  684.4 1.0 maximum_select_fusion.1
  685.5 0.3 collective-permute-start.2
  685.8 11.4 %convolution_add_fusion = f32[1024,128]{0,1:T(8,128)S(1)} fusion(f32[1024,128]{0,1:T(8,128)S(1)} %copy.17, bf16[1024,8192]{1,0:T(8,128)(2,1)} %all-gather.2.cloned.1.call-done, bf16[8192,128]{1,0:T(8,128)(2,1)S(1)} %copy-done), kind=kOutput, calls=%fused_computation.12 | convolution fusion | flops 2147614720 | bytes 19922944 | tf_op jit(solution)/shard_map/dot_general | solution.py:89
  697.2 1.2 maximum_select_fusion
  698.5 1.2 fusion.18
  699.8 0.2 copy.15
  700.0 0.2 copy.16
  700.2 6.7 while.11
  700.2 0.6 dynamic_slice.26
  701.6 0.8 fusion.41
  702.4 0.5 fusion.42
  702.9 0.6 fusion.43
  703.5 0.6 dynamic_slice.26
  704.9 0.8 fusion.41
  705.7 0.5 fusion.42
  706.2 0.6 fusion.43
  706.8 0.7 copy-done.7
  (33 shorter events, 0.5 us)
Async XLA Ops:
  6.5 679.2 %copy-start = (bf16[8192,128]{1,0:T(8,128)(2,1)S(1)}, bf16[8192,128]{1,0:T(8,128)(2,1)}, u32[]{:S(2)}) copy-start(bf16[8192,128]{1,0:T(8,128)(2,1)} %param.10) | copy-start | bytes 6291460
  6.5 20.9 %copy-start.1 = (bf16[1024,128]{1,0:T(8,128)(2,1)S(1)}, bf16[1024,128]{1,0:T(8,128)(2,1)}, u32[]{:S(2)}) copy-start(bf16[1024,128]{1,0:T(8,128)(2,1)} %param.9) | copy-start | bytes 786436
  6.5 8.3 %copy-start.3 = (bf16[16,32,128]{2,1,0:T(8,128)(2,1)S(1)}, bf16[16,32,128]{2,1,0:T(8,128)(2,1)}, u32[]{:S(2)}) copy-start(bf16[16,32,128]{2,1,0:T(8,128)(2,1)} %param.13) | copy-start | bytes 393220
  6.5 19.1 %copy-start.5 = (s32[8]{0:T(128)S(1)}, s32[8]{0:T(128)}, u32[]{:S(2)}) copy-start(s32[8]{0:T(128)} %param.15) | copy-start | bytes 100
  6.5 20.3 %copy-start.4 = (s32[1024]{0:T(1024)S(1)}, s32[1024]{0:T(1024)}, u32[]{:S(2)}) copy-start(s32[1024]{0:T(1024)} %param.14) | copy-start | bytes 12292
  6.5 351.8 %all-gather.2.cloned.1.call-start = ((), (), s32[]{:S(2)}) async-start(), calls=%async_computation.1 | async-start | bytes 17039360 | tf_op jit(solution)/shard_map/all_gather | solution.py:88
  9.1 17.8 %all-to-all-start = ((bf16[4,16,128,32]{2,3,1,0:T(8,128)(2,1)}), bf16[4,16,128,32]{2,3,1,0:T(8,128)(2,1)S(1)}, u32[]{:S(2)}, u32[]{:S(2)}) async-start(bf16[4,16,128,32]{2,3,1,0:T(8,128)(2,1)} %stack.2), calls=%async_computation | async-start | bytes 1048576 | tf_op jit(solution)/shard_map/all_to_all | solution.py:16
  27.7 650.2 %copy-start.2 = (bf16[8,32,128]{2,1,0:T(8,128)(2,1)S(1)}, bf16[8,32,128]{2,1,0:T(8,128)(2,1)}, u32[]{:S(2)}) copy-start(bf16[8,32,128]{2,1,0:T(8,128)(2,1)} %gather_fusion.1) | copy-start | bytes 196612
  369.2 308.5 %collective-permute-start = (bf16[1024,32]{0,1:T(8,128)(2,1)S(1)}, bf16[1024,32]{0,1:T(8,128)(2,1)S(1)}, u32[]{:S(2)}, u32[]{:S(2)}) collective-permute-start(bf16[1024,32]{0,1:T(8,128)(2,1)S(1)} %convolution_convert_fusion.1), channel_id=1, source_target_pairs={{0,1},{1,0},{2,3},{3,2},{4,5},{5,4},{6,7},{7,6},{8,9},{9,8},{10,11... | collective-permute-start | bytes 196616 | tf_op jit(solution)/shard_map/ppermute | solution.py:27
  677.8 6.7 collective-permute-start.1
  685.5 11.7 %collective-permute-start.2 = (bf16[1024,128]{0,1:T(8,128)(2,1)S(1)}, bf16[1024,128]{0,1:T(8,128)(2,1)}, u32[]{:S(2)}, u32[]{:S(2)}) collective-permute-start(bf16[1024,128]{0,1:T(8,128)(2,1)S(1)} %maximum_select_fusion.1), channel_id=1, source_target_pairs={{0,4},{4,0},{1,5},{5,1},{2,6},{6,2},{3,7},{7,3},{8,12},{12,8},{9,1... | collective-permute-start | bytes 786440 | tf_op jit(solution)/shard_map/ppermute | solution.py:27
  698.5 1.7 copy-start.6
  706.8 0.7 copy-start.7
Sparse Core Ops, SparseCore 0:
  9.1 349.2 all-gather.1
